TPU v7x, 32 devices: a whole 2x2x4 slice. The times are simulated.
32 devices in a mesh: dp: 4 (over z), ctx: 2 (over x), hidden: 4 (over y, core).
Axes of the slice: x: 2, y: 2, z: 4, core: 2. Of those that a mesh axis runs over, the one named last changes fastest.
Arguments:
- activations: bfloat16 [4, 1024, 53248], P('dp', 'ctx', 'hidden'), may hold values from -6 to 6
- out_grads: bfloat16 [4, 1024, 16384], P('dp', 'ctx', 'hidden'), may hold values from -0.1875 to 0.1875
- input_basis: bfloat16 [53248, 512], P('hidden', ('dp', 'ctx')), may hold values from -0.02734375 to 0.02734375
- output_basis: bfloat16 [16384, 512], P('hidden', ('dp', 'ctx')), may hold values from -0.046875 to 0.046875
- rotation: bfloat16 [512, 512], P('ctx'), may hold values from -0.25 to 0.25
Outputs:
- logged: float32 [4, 512, 512], P('dp', 'ctx', 'hidden')
All inputs are finite; a program needn't handle non-finite values.
Results may differ from a plain program's by a relative error of at most 0.0049.
Values may be sent and summed in bfloat16 or wider, within the bound.
A program may use at most 64 MiB of HBM per device.

v0:
```python
import jax
import jax.numpy as jnp
from jax import lax
from jax.sharding import PartitionSpec as P


def outer_sum(left, right):
    return lax.dot_general(
        left, right, (((0,), (0,)), ((), ())), preferred_element_type=jnp.float32
    )


def local(activations, out_grads, input_basis, output_basis, rotation):
    tokens = activations.reshape(-1, activations.shape[-1])
    grad_rows = out_grads.reshape(-1, out_grads.shape[-1])
    in_part = jnp.dot(
        tokens,
        lax.all_gather(input_basis, ("dp", "ctx"), axis=1, tiled=True),
        preferred_element_type=jnp.float32,
    )
    out_part = jnp.dot(
        grad_rows,
        lax.all_gather(output_basis, ("dp", "ctx"), axis=1, tiled=True),
        preferred_element_type=jnp.float32,
    )
    in_cols = lax.psum_scatter(in_part, "hidden", scatter_dimension=1, tiled=True).astype(
        jnp.bfloat16
    )
    out_side = lax.psum(out_part, "hidden")
    out_side = out_side.astype(jnp.bfloat16)
    total = lax.psum(outer_sum(out_side, in_cols), "ctx")
    lowrank = total.astype(jnp.bfloat16)
    logged = jnp.dot(rotation, lowrank, preferred_element_type=jnp.float32)
    return logged.reshape(1, logged.shape[0], logged.shape[1])


def solution(mesh):
    return jax.shard_map(
        local,
        mesh=mesh,
        in_specs=(
            P("dp", "ctx", "hidden"),
            P("dp", "ctx", "hidden"),
            P("hidden", ("dp", "ctx")),
            P("hidden", ("dp", "ctx")),
            P("ctx", None),
        ),
        out_specs=P("dp", "ctx", "hidden"),
        check_vma=False,
    )
```

profile of v0, /device:TPU:5, one launch (start us, length us, event | category | flops | bytes accessed | tf_op | source)
XLA Modules:
  0.0 325.8 jit_solution(16970726115371257310)
XLA Ops:
  6.5 0.0 copy-start
  6.5 0.0 all-gather.5.cloned.1.call-start
  6.5 0.7 all-gather.5.cloned.1.call-update
  7.3 0.0 all-gather.3.cloned.1.call-start
  7.3 0.7 all-gather.3.cloned.1.call-update
  8.0 0.0 reduce-scatter.2.cloned.1.call-start
  8.1 190.9 %all-gather.5.cloned.1.call-done = bf16[13312,512]{0,1:T(8,128)(2,1)} async-done(((bf16[13312,64]{0,1:T(8,128)(2,1)}), bf16[13312,512]{0,1:T(8,128)(2,1)}) %all-gather.5.cloned.1.call-update) | async-done | bytes 13631504 | tf_op jit(solution)/shard_map/all_gather | solution.py:18
  198.9 15.1 %fusion = f32[512,512]{1,0:T(8,128)} fusion(bf16[13312,512]{0,1:T(8,128)(2,1)} %all-gather.5.cloned.1.call-done, bf16[1,512,13312]{2,1,0:T(8,128)(2,1)} %param.5), kind=kOutput, calls=%fused_computation | convolution fusion | flops 6979321856 | bytes 28311552 | tf_op jit(solution)/shard_map/dot_general | solution.py:16
  214.1 0.0 reduce-scatter.2.cloned.1.call-update
  214.1 57.5 %all-gather.3.cloned.1.call-done = bf16[4096,512]{0,1:T(8,128)(2,1)} async-done(((bf16[4096,64]{0,1:T(8,128)(2,1)}), bf16[4096,512]{0,1:T(8,128)(2,1)}) %all-gather.3.cloned.1.call-update) | async-done | bytes 4194320 | tf_op jit(solution)/shard_map/all_gather | solution.py:23
  271.6 5.8 %fusion.2 = f32[512,512]{1,0:T(8,128)S(1)} fusion(bf16[4096,512]{0,1:T(8,128)(2,1)} %all-gather.3.cloned.1.call-done, bf16[1,512,4096]{2,1,0:T(8,128)(2,1)} %param.6), kind=kOutput, calls=%fused_computation.2 | convolution fusion | flops 2147483648 | bytes 9437184 | tf_op jit(solution)/shard_map/dot_general | solution.py:21
  277.4 29.4 %all-reduce.2 = bf16[512,512]{1,0:T(8,128)(2,1)S(1)} all-reduce(f32[512,512]{1,0:T(8,128)S(1)} %fusion.2), channel_id=1, replica_groups=mesh['dp'=4,'ctx'=2,'hidden'=4] {'hidden'}, use_global_device_ids=true, to_apply=%region_0.0 | all-reduce | flops 262144 | bytes 1572864 | tf_op jit(solution)/shard_map/psum | solution.py:29
  306.8 0.0 reduce-scatter.2.cloned.1.call-done
  306.8 1.3 fusion.4
  308.1 10.2 %all-reduce.3 = bf16[512,128]{1,0:T(8,128)(2,1)S(1)} all-reduce(f32[512,128]{1,0:T(8,128)S(1)} %fusion.4), channel_id=1, replica_groups=mesh['dp'=4,'ctx'=2,'hidden'=4] {'ctx'}, use_global_device_ids=true, to_apply=%region_2.0 | all-reduce | flops 65536 | bytes 393216 | tf_op jit(solution)/shard_map/psum | solution.py:31
  318.2 0.0 copy-done
  318.3 0.2 convolution_bitcast_fusion
  318.5 0.8 copy.6
Async XLA Ops:
  6.5 311.7 %copy-start = (bf16[256,512]{1,0:T(8,128)(2,1)S(1)}, bf16[256,512]{1,0:T(8,128)(2,1)}, u32[]{:S(2)}) copy-start(bf16[256,512]{1,0:T(8,128)(2,1)} %param.9) | copy-start | bytes 786436
  6.5 192.4 %all-gather.5.cloned.1.call-start = ((), (), s32[]{:S(2)}) async-start(), calls=%async_computation.2 | async-start | bytes 15335424 | tf_op jit(solution)/shard_map/all_gather | solution.py:18
  7.3 264.3 %all-gather.3.cloned.1.call-start = ((), (), s32[]{:S(2)}) async-start(), calls=%async_computation.1 | async-start | bytes 4718592 | tf_op jit(solution)/shard_map/all_gather | solution.py:23
  8.0 298.8 %reduce-scatter.2.cloned.1.call-start = ((), (), s32[]{:S(2)}) async-start(), calls=%async_computation.3 | async-start | bytes 1310720 | tf_op jit(solution)/shard_map/reduce_scatter | solution.py:26
Sparse Core Ops, SparseCore 0:
  9.5 189.3 all-gather.4
  201.0 70.4 all-gather.2
  274.1 27.1 reduce-scatter.1
where the time goes:
time: 330 us; the launch traced here: 326 us
  waiting for transfers between devices  250 us (76%)
  blocking collectives  39.5 us (12%)
  matrix products  22.5 us (7%)
  between operations  13.2 us (4%)
    all_gather x1, waiting for transfers between devices, local(): lax.all_gather(input_basis, ('dp', 'ctx'), axis=1, tiled=True)  191 us
    all_gather x1, waiting for transfers between devices, local(): lax.all_gather(output_basis, ('dp', 'ctx'), axis=1, tiled=True)  57.5 us
    psum x1, blocking collectives, local(): out_side = lax.psum(out_part, 'hidden')  29.4 us
    dot_general x1, matrix products, local(): jnp.dot(tokens, lax.all_gather(input_basis, ('dp', 'ctx'), axis=1, tiled=...  15.1 us
    psum x1, blocking collectives, local(): total = lax.psum(outer_sum(out_side, in_cols), 'ctx')  10.2 us
  transfers between devices with their start and end apart: 3, of which 2 were waited for; matrix products, arithmetic and copies ran while one was open for 6% of the time, Pallas kernels for 0%

commit v1 on v0

--- a/solution.py
+++ b/solution.py
@@ -1,7 +1,17 @@
+import functools
+
 import jax
 import jax.numpy as jnp
 from jax import lax
+from jax.experimental import pallas as pl
+from jax.experimental.pallas import tpu as pltpu
 from jax.sharding import PartitionSpec as P
+
+MESH = pl.DeviceIdType.MESH
+NT = (((1,), (1,)), ((), ()))
+CHUNK = 1024
+NZ = 4
+LAG = 1
 
 
 def outer_sum(left, right):
@@ -34,17 +44,354 @@
     return logged.reshape(1, logged.shape[0], logged.shape[1])
 
 
+def kernel(
+    n_out, n_in, n_a,
+    act_hbm, grad_hbm, bi_hbm, bo_hbm, rot_ref, out_ref,
+    G, T, acc, RO, RI, OS, IS,
+    load_sem, own_sem, g_recv, g_send,
+    ro_recv, ro_send, ri_recv, ri_send,
+    os_recv, os_send, osr_send, is_sem,
+):
+    z, x, h = lax.axis_index("dp"), lax.axis_index("ctx"), lax.axis_index("hidden")
+    nc = n_out + n_in
+    nb = nc - n_a
+    w = bi_hbm.shape[0]
+    d_out = grad_hbm.shape[1]
+    d_in = act_hbm.shape[1]
+    z_last = jnp.where(z < 2, NZ - 1, 0)
+
+    def rows(xx):
+        return pl.ds(pl.multiple_of(xx * w, w), w)
+
+    def lanes(c):
+        return pl.ds(pl.multiple_of(c * CHUNK, CHUNK), CHUNK)
+
+    own_in = pltpu.make_async_copy(
+        bi_hbm, G.at[z, rows(x), pl.ds(d_out, d_in)], own_sem.at[0])
+    own_out = pltpu.make_async_copy(
+        bo_hbm, G.at[z, rows(x), pl.ds(0, d_out)], own_sem.at[1])
+    own_out.start()
+    own_in.start()
+
+    barrier = pltpu.get_barrier_semaphore()
+    pl.semaphore_signal(barrier, inc=1, device_id={"ctx": 1 - x}, device_id_type=MESH)
+    for k in range(1, NZ):
+        pl.semaphore_signal(
+            barrier, inc=1, device_id={"hidden": lax.rem(h + k, NZ)}, device_id_type=MESH)
+
+    @pl.when(z > 0)
+    def _():
+        pl.semaphore_signal(barrier, inc=1, device_id={"dp": z - 1}, device_id_type=MESH)
+
+    @pl.when(z < NZ - 1)
+    def _():
+        pl.semaphore_signal(barrier, inc=1, device_id={"dp": z + 1}, device_id_type=MESH)
+
+    pl.semaphore_wait(
+        barrier, NZ + jnp.where(z > 0, 1, 0) + jnp.where(z < NZ - 1, 1, 0))
+
+    def piece(way, zs, xx, c):
+        dev = ({"dp": z + 1}, {"dp": z - 1}, {"ctx": 1 - x})[way]
+        ref = G.at[zs, rows(xx), lanes(c)]
+        return pltpu.make_async_remote_copy(
+            src_ref=ref, dst_ref=ref, send_sem=g_send.at[way, zs, xx],
+            recv_sem=g_recv.at[zs, xx, c], device_id=dev, device_id_type=MESH)
+
+    def bulk(way, zs, xx, first, count):
+        dev = ({"dp": z + 1}, {"dp": z - 1}, {"ctx": 1 - x})[way]
+        ref = G.at[zs, rows(xx), pl.ds(first * CHUNK, count * CHUNK)]
+        return pltpu.make_async_remote_copy(
+            src_ref=ref, dst_ref=ref, send_sem=g_send.at[way, zs, xx],
+            recv_sem=g_recv.at[zs, xx, 0], device_id=dev, device_id_type=MESH)
+
+    own_out.wait()
+    own_in.wait()
+
+    def first_sends(i, carry):
+        @pl.when(z < NZ - 1)
+        def _():
+            piece(0, z, x, i).start()
+
+        @pl.when(z > 0)
+        def _():
+            piece(1, z, x, i).start()
+
+        piece(2, z, x, jnp.where(i < n_a, nb + i, i - n_a)).start()
+        return carry
+
+    lax.fori_loop(0, nc, first_sends, 0)
+
+    load_out = pltpu.make_async_copy(grad_hbm, T.at[:, pl.ds(0, d_out)], load_sem.at[0])
+    load_in = pltpu.make_async_copy(act_hbm, T.at[:, pl.ds(d_out, d_in)], load_sem.at[1])
+    load_out.start()
+    load_in.start()
+    acc[...] = jnp.zeros_like(acc)
+    load_out.wait()
+    load_in.wait()
+
+    def multiply(zs, c):
+        side = jnp.where(c < n_out, 0, 1)
+        acc[side, zs] += lax.dot_general(
+            G[zs, :, lanes(c)], T[:, lanes(c)], NT, preferred_element_type=jnp.float32)
+
+    per_round = nc + n_a
+
+    def z_step(t):
+        r, i = lax.div(t, per_round) + 1, lax.rem(t, per_round)
+        c = jnp.where(i < nc, i, i - n_a)
+        xx = jnp.where(i < nc, x, 1 - x)
+        for up in (True, False):
+            zs = z + r if up else z - r
+
+            @pl.when((zs < NZ) if up else (zs >= 0))
+            def _(zs=zs, up=up):
+                piece(0, zs, xx, c).wait_recv()
+                if up:
+                    @pl.when(z > 0)
+                    def _():
+                        piece(1, zs, xx, c).start()
+                else:
+                    @pl.when(z < NZ - 1)
+                    def _():
+                        piece(0, zs, xx, c).start()
+
+                @pl.when(i < nb)
+                def _():
+                    piece(2, zs, xx, c).start()
+
+                @pl.when(i >= nc)
+                def _():
+                    multiply(zs, c)
+
+    n_units = nc + (NZ - 1) * nb
+
+    def unit(n):
+        m = n - nc
+        ends = (z == 0) | (z == NZ - 1)
+        r = lax.div(m, nb) + 1
+        z_end, c_end = jnp.where(z == 0, r, NZ - 1 - r), lax.rem(m, nb)
+        near = m < 2 * nb
+        z_mid = jnp.where(near, jnp.where(lax.rem(m, 2) == 0, z + 1, z - 1), z_last)
+        c_mid = jnp.where(near, lax.div(m, 2), m - 2 * nb)
+        own = n < nc
+        zs = jnp.where(own, z, jnp.where(ends, z_end, z_mid))
+        c = jnp.where(
+            own, jnp.where(n < n_a, nb + n, n - n_a), jnp.where(ends, c_end, c_mid))
+        return zs, c
+
+    def x_step(n):
+        zs, c = unit(n)
+        piece(2, zs, 1 - x, c).wait_recv()
+
+        @pl.when(n < n_a)
+        def _():
+            @pl.when(z < NZ - 1)
+            def _():
+                piece(0, z, 1 - x, c).start()
+
+            @pl.when(z > 0)
+            def _():
+                piece(1, z, 1 - x, c).start()
+
+        multiply(zs, c)
+
+    def part(side, to, frm):
+        buf, ssem, rsem = ((RO, ro_send, ro_recv), (RI, ri_send, ri_recv))[side]
+        return pltpu.make_async_remote_copy(
+            src_ref=acc.at[side, to], dst_ref=buf.at[frm], send_sem=ssem.at[to],
+            recv_sem=rsem.at[frm], device_id={"hidden": to}, device_id_type=MESH)
+
+    def send_parts(side, last):
+        for to in range(NZ):
+            @pl.when((h != to) & ((z_last == to) if last else (z_last != to)))
+            def _(to=to):
+                part(side, to, h).start()
+
+    def summed(side):
+        buf = RI if side else RO
+        value = acc[side, h]
+        for k in range(1, NZ):
+            frm = lax.rem(h + k, NZ)
+            part(side, h, frm).wait_recv()
+            value = value + buf[frm]
+        return value.astype(jnp.bfloat16)
+
+    blk = acc.shape[2]
+
+    def block_of(hh):
+        return pl.ds(pl.multiple_of(hh * blk, blk), blk)
+
+    def os_copy(xx, hh, dev, sem):
+        ref = OS.at[xx, block_of(hh), :]
+        return pltpu.make_async_remote_copy(
+            src_ref=ref, dst_ref=ref, send_sem=sem, recv_sem=os_recv.at[xx, hh],
+            device_id=dev, device_id_type=MESH)
+
+    def is_copy(xx):
+        return pltpu.make_async_remote_copy(
+            src_ref=IS.at[xx], dst_ref=IS.at[xx], send_sem=is_sem.at[0],
+            recv_sem=is_sem.at[1], device_id={"ctx": 1 - x}, device_id_type=MESH)
+
+    def finish_in():
+        IS[x] = summed(1)
+        is_copy(x).start()
+
+    out_early = nc + 2 * nb - (nb - n_out)
+    in_early = nc + 2 * nb
+    out_late = nc + 2 * nb + n_out
+    step_1 = out_late + 4
+    step_2 = step_1 + 3
+
+    def stages(n):
+        @pl.when(n == out_early)
+        def _():
+            send_parts(0, False)
+
+        @pl.when(n == in_early)
+        def _():
+            send_parts(1, False)
+
+        @pl.when(n == out_late)
+        def _():
+            send_parts(0, True)
+
+        @pl.when(n == step_1)
+        def _():
+            OS[x, block_of(h), :] = summed(0)
+            os_copy(x, h, {"ctx": 1 - x}, os_send.at[0]).start()
+            for k in range(1, NZ):
+                os_copy(x, h, {"hidden": lax.rem(h + k, NZ)}, os_send.at[k]).start()
+
+            @pl.when(h != z_last)
+            def _():
+                finish_in()
+
+        @pl.when(n == step_2)
+        def _():
+            os_copy(1 - x, h, {"ctx": 1 - x}, os_send.at[0]).wait_recv()
+            for k in range(1, NZ):
+                os_copy(1 - x, h, {"hidden": lax.rem(h + k, NZ)}, osr_send.at[k - 1]).start()
+
+    n_z = per_round * (NZ - 1)
+
+    def body(t, carry):
+        @pl.when(t < n_z)
+        def _():
+            z_step(t)
+
+        n = t - LAG
+
+        @pl.when((n >= 0) & (n < n_units))
+        def _():
+            x_step(n)
+
+        stages(n)
+        return carry
+
+    lax.fori_loop(0, max(n_z, n_units + LAG), body, 0)
+
+    send_parts(1, True)
+
+    @pl.when(h == z_last)
+    def _():
+        finish_in()
+
+    for k in range(1, NZ):
+        for xx in range(2):
+            os_copy(xx, lax.rem(h + k, NZ), {"ctx": 1 - x}, os_send.at[0]).wait_recv()
+
+    total = lax.dot_general(OS[x], IS[x], NT, preferred_element_type=jnp.float32)
+    is_copy(1 - x).wait_recv()
+    total = total + lax.dot_general(OS[1 - x], IS[1 - x], NT, preferred_element_type=jnp.float32)
+    out_ref[...] = jnp.dot(
+        rot_ref[...], total.astype(jnp.bfloat16), preferred_element_type=jnp.float32)
+
+    is_copy(x).wait_send()
+    for k in range(NZ):
+        os_copy(x, h, {"ctx": 1 - x}, os_send.at[k]).wait_send()
+        if k:
+            os_copy(x, h, {"ctx": 1 - x}, osr_send.at[k - 1]).wait_send()
+    for to in range(NZ):
+        @pl.when(h != to)
+        def _(to=to):
+            part(0, to, h).wait_send()
+            part(1, to, h).wait_send()
+    for zs in range(NZ):
+        for way, sends in ((0, (z < NZ - 1) & (zs <= z)), (1, (z > 0) & (zs >= z))):
+            @pl.when(sends)
+            def _(way=way, zs=zs):
+                bulk(way, zs, x, 0, nc).wait_send()
+                bulk(way, zs, 1 - x, nb, n_a).wait_send()
+
+        @pl.when(zs == z)
+        def _(zs=zs):
+            bulk(2, zs, x, 0, nc).wait_send()
+
+        @pl.when(zs != z)
+        def _(zs=zs):
+            bulk(2, zs, x, 0, nb).wait_send()
+
+
+def fast(activations, out_grads, input_basis, output_basis, rotation):
+    tokens = activations.reshape(-1, activations.shape[-1])
+    grad_rows = out_grads.reshape(-1, out_grads.shape[-1])
+    d_in, d_out = tokens.shape[1], grad_rows.shape[1]
+    width = d_in + d_out
+    m = tokens.shape[0]
+    w = input_basis.shape[1]
+    rank = rotation.shape[1]
+    blk = 2 * w
+    n_out, n_in = d_out // CHUNK, d_in // CHUNK
+    nc = n_out + n_in
+    n_a = max(1, round(0.18 * nc))
+    dma = pltpu.SemaphoreType.DMA
+    f32, bf16 = jnp.float32, jnp.bfloat16
+    anym = pl.BlockSpec(memory_space=pl.ANY)
+    vmem = pl.BlockSpec(memory_space=pltpu.VMEM)
+    logged = pl.pallas_call(
+        functools.partial(kernel, n_out, n_in, n_a),
+        out_shape=jax.ShapeDtypeStruct((rotation.shape[0], blk), f32),
+        in_specs=[anym, anym, anym, anym, vmem],
+        out_specs=vmem,
+        scratch_shapes=[
+            pltpu.VMEM((NZ, blk, width), bf16),
+            pltpu.VMEM((m, width), bf16),
+            pltpu.VMEM((2, NZ, blk, m), f32),
+            pltpu.VMEM((NZ, blk, m), f32),
+            pltpu.VMEM((NZ, blk, m), f32),
+            pltpu.VMEM((2, rank, m), bf16),
+            pltpu.VMEM((2, blk, m), bf16),
+            dma((2,)), dma((2,)), dma((NZ, 2, nc)), dma((3, NZ, 2)),
+            dma((NZ,)), dma((NZ,)), dma((NZ,)), dma((NZ,)),
+            dma((2, NZ)), dma((NZ,)), dma((NZ,)), dma((2,)),
+        ],
+        compiler_params=pltpu.CompilerParams(
+            collective_id=0, has_side_effects=True, vmem_limit_bytes=60 * 2**20),
+    )(tokens, grad_rows, input_basis.T, output_basis.T, rotation)
+    return logged.reshape(1, logged.shape[0], logged.shape[1])
+
+
 def solution(mesh):
-    return jax.shard_map(
-        local,
-        mesh=mesh,
-        in_specs=(
-            P("dp", "ctx", "hidden"),
-            P("dp", "ctx", "hidden"),
-            P("hidden", ("dp", "ctx")),
-            P("hidden", ("dp", "ctx")),
-            P("ctx", None),
-        ),
-        out_specs=P("dp", "ctx", "hidden"),
-        check_vma=False,
-    )
+    size = mesh.shape
+
+    def program(activations, out_grads, input_basis, output_basis, rotation):
+        fits = (
+            size["dp"] == NZ and size["hidden"] == NZ and size["ctx"] == 2
+            and activations.shape[2] % (CHUNK * size["hidden"]) == 0
+            and out_grads.shape[2] % (CHUNK * size["hidden"]) == 0
+        )
+        return jax.shard_map(
+            fast if fits else local,
+            mesh=mesh,
+            in_specs=(
+                P("dp", "ctx", "hidden"),
+                P("dp", "ctx", "hidden"),
+                P("hidden", ("dp", "ctx")),
+                P("hidden", ("dp", "ctx")),
+                P("ctx", None),
+            ),
+            out_specs=P("dp", "ctx", "hidden"),
+            check_vma=False,
+        )(activations, out_grads, input_basis, output_basis, rotation)
+
+    return program

time: 330 us -> 195 us (0.59)
  waiting for transfers between devices: 250 us -> 0 us
  Pallas kernels: 0 us -> 191 us
  blocking collectives: 39.5 us -> 0 us
  matrix products: 22.5 us -> 0 us
  between operations: 13.2 us -> 0.01 us
    all_gather x2 -> x0, waiting for transfers between devices: 248 us -> none  [the longest x1 191 us: local(): lax.all_gather(input_basis, ('dp', 'ctx'), axis=1, tiled=True)]
    pallas_call x0 -> x1, Pallas kernels: none -> 191 us  [fast(): pl.pallas_call(functools.partial(kernel, n_out, n_in, n_a), out_shape=jax...]
    psum x2 -> x0, blocking collectives: 39.5 us -> none  [the longest x1 29.4 us: local(): out_side = lax.psum(out_part, 'hidden')]
    dot_general x4 -> x0, matrix products: 22.5 us -> none  [the longest x1 15.1 us: local(): jnp.dot(tokens, lax.all_gather(input_basis, ('dp', 'ctx'), axis=1, tiled=...]
  transfers between devices with their start and end apart: 3 -> 0, of which waited for: 2 -> 0; matrix products, arithmetic and copies ran while one was open for 6% -> 0% of each run, Pallas kernels for 0% -> 0%
where the time goes in v1:
time: 195 us; the launch traced here: 193 us
  Pallas kernels  191 us (98%)
    pallas_call x1, Pallas kernels, fast(): pl.pallas_call(functools.partial(kernel, n_out, n_in, n_a), out_shape=jax...  191 us

profile of v1, /device:TPU:5, one launch (start us, length us, event | category | flops | bytes accessed | tf_op | source)
XLA Modules:
  0.0 192.9 jit_solution(10262978910505026231)
XLA Ops:
  0.0 191.3 %shard_map.55 = f32[256,128]{1,0:T(8,128)} custom-call(bf16[512,13312]{1,0:T(8,128)(2,1)} %bitcast.5, bf16[512,4096]{1,0:T(8,128)(2,1)} %bitcast.6, bf16[64,13312]{1,0:T(8,128)(2,1)} %bitcast.7, bf16[64,4096]{1,0:T(8,128)(2,1)} %bitcast.9, bf16[256,512]{1,0:T(8,128)(2,1)} %rot_ref.1), custom_call_target="tpu_custom_call" | custom-call | tf_op jit(solution)/shard_map/pallas_call | solution.py:351
  191.3 1.6 copy.7

commit v2 on v1

v2 whole, which is shorter than its diff:
```python
import jax
import jax.numpy as jnp
from jax import lax
from jax.experimental import pallas as pl
from jax.experimental.pallas import tpu as pltpu
from jax.sharding import PartitionSpec as P

MESH = pl.DeviceIdType.MESH
NT = (((1,), (1,)), ((), ()))
NZ = 4
NC = 17
M0 = 9
N_M = 3
K0 = 12
N_K = 3
A0 = 15
N_A = 2
N_W = N_M + N_K
N_B = K0
N_E = NC - N_K
OUT_AT = 8
N_OUT = 4
LAG = 1
DELAY = 18
PAUSE, HOLD = 35, 4
OUT_EARLY, HELP, OUT_LATE, OTHER_A, OUT_SUM, IN_EARLY, OUT_RELAY = 34, 42, 43, 45, 47, 48, 50


def outer_sum(left, right):
    return lax.dot_general(
        left, right, (((0,), (0,)), ((), ())), preferred_element_type=jnp.float32
    )


def local(activations, out_grads, input_basis, output_basis, rotation):
    tokens = activations.reshape(-1, activations.shape[-1])
    grad_rows = out_grads.reshape(-1, out_grads.shape[-1])
    in_part = jnp.dot(
        tokens,
        lax.all_gather(input_basis, ("dp", "ctx"), axis=1, tiled=True),
        preferred_element_type=jnp.float32,
    )
    out_part = jnp.dot(
        grad_rows,
        lax.all_gather(output_basis, ("dp", "ctx"), axis=1, tiled=True),
        preferred_element_type=jnp.float32,
    )
    in_cols = lax.psum_scatter(in_part, "hidden", scatter_dimension=1, tiled=True).astype(
        jnp.bfloat16
    )
    out_side = lax.psum(out_part, "hidden")
    out_side = out_side.astype(jnp.bfloat16)
    total = lax.psum(outer_sum(out_side, in_cols), "ctx")
    lowrank = total.astype(jnp.bfloat16)
    logged = jnp.dot(rotation, lowrank, preferred_element_type=jnp.float32)
    return logged.reshape(1, logged.shape[0], logged.shape[1])


def kernel(
    act_hbm, grad_hbm, bi_hbm, bo_hbm, rot_ref, out_ref,
    G, T, acc, RO, RI, OS, IS, TN, PA, PS, PR,
    load_sem, own_sem, g_recv, g_send,
    ro_recv, ro_send, ri_recv, ri_send,
    os_recv, os_send, osr_send, is_sem,
    t_recv, t_send, p_recv, p_send,
):
    z, x, h = lax.axis_index("dp"), lax.axis_index("ctx"), lax.axis_index("hidden")
    chunk = G.shape[2] // NC
    w = bi_hbm.shape[0]
    d_out = grad_hbm.shape[1]
    d_in = act_hbm.shape[1]
    head = OUT_AT * chunk
    low = z < 2
    end = (z == 0) | (z == NZ - 1)
    mid = jnp.logical_not(end)
    z_last = jnp.where(low, NZ - 1, 0)
    inward = jnp.where(low, z + 1, z - 1)
    outward = jnp.where(low, 0, NZ - 1)
    far = z_last

    def rows(xx):
        return pl.ds(pl.multiple_of(xx * w, w), w)

    def lanes(c):
        return pl.ds(pl.multiple_of(c * chunk, chunk), chunk)

    def local_parts(src_in, src_out, dst, sem):
        return (
            pltpu.make_async_copy(src_out, dst(head, d_out), sem.at[0]),
            pltpu.make_async_copy(src_in.at[:, pl.ds(0, head)], dst(0, head), sem.at[1]),
            pltpu.make_async_copy(
                src_in.at[:, pl.ds(head, d_in - head)],
                dst(head + d_out, d_in - head), sem.at[2]),
        )

    own = local_parts(
        bi_hbm, bo_hbm, lambda a, n: G.at[z, rows(x), pl.ds(a, n)], own_sem)
    load = local_parts(act_hbm, grad_hbm, lambda a, n: T.at[:, pl.ds(a, n)], load_sem)
    for copy in own:
        copy.start()

    barrier = pltpu.get_barrier_semaphore()
    pl.semaphore_signal(barrier, inc=1, device_id={"ctx": 1 - x}, device_id_type=MESH)
    pl.semaphore_signal(barrier, inc=1, device_id={"dp": inward}, device_id_type=MESH)
    for k in range(1, NZ):
        pl.semaphore_signal(
            barrier, inc=1, device_id={"hidden": lax.rem(h + k, NZ)}, device_id_type=MESH)

    @pl.when(mid)
    def _():
        pl.semaphore_signal(barrier, inc=1, device_id={"dp": outward}, device_id_type=MESH)

    pl.semaphore_wait(barrier, NZ + 1 + jnp.where(mid, 1, 0))

    def device(way):
        return ({"dp": inward}, {"dp": outward}, {"ctx": 1 - x})[way]

    def piece(way, zs, xx, c):
        ref = G.at[zs, rows(xx), lanes(c)]
        return pltpu.make_async_remote_copy(
            src_ref=ref, dst_ref=ref, send_sem=g_send.at[way, zs, xx],
            recv_sem=g_recv.at[zs, xx, c], device_id=device(way), device_id_type=MESH)

    def sent(way, zs, xx, first, stop):
        ref = G.at[zs, rows(xx), pl.ds(first * chunk, (stop - first) * chunk)]
        pltpu.make_async_remote_copy(
            src_ref=ref, dst_ref=ref, send_sem=g_send.at[way, zs, xx],
            recv_sem=g_recv.at[zs, xx, 0], device_id=device(way), device_id_type=MESH,
        ).wait_send()

    def arrived(zs, xx, c):
        piece(2, zs, xx, c).wait_recv()

    def plain(i):
        return jnp.where(i == 0, OUT_AT, i - 1)

    def order_all(i):
        return jnp.where(
            i < N_K, K0 + i,
            jnp.where(i < N_K + N_M, M0 + i - N_K,
                      jnp.where(i < A0, plain(i - N_K - N_M), i)))

    def order_kept(i):
        return order_all(i + N_K)

    for copy in own:
        copy.wait()
    for copy in load:
        copy.start()

    def first_sends(i, carry):
        piece(0, z, x, order_all(i)).start()

        @pl.when(mid)
        def _():
            @pl.when(i < N_E)
            def _():
                piece(1, z, x, order_kept(i)).start()

            piece(2, z, x, jnp.where(i < N_A, A0 + i, order_all(i - N_A))).start()

        @pl.when(end & (i < N_E))
        def _():
            piece(2, z, x, jnp.where(i < N_A, A0 + i, order_kept(i - N_A))).start()

        return carry

    lax.fori_loop(0, NC, first_sends, 0)

    def t_copy(k):
        return pltpu.make_async_remote_copy(
            src_ref=T.at[:, pl.ds((K0 + k) * chunk, chunk)],
            dst_ref=TN.at[:, pl.ds(k * chunk, chunk)],
            send_sem=t_send.at[k], recv_sem=t_recv.at[k],
            device_id=device(0), device_id_type=MESH)

    acc[...] = jnp.zeros_like(acc)
    for copy in load:
        copy.wait()

    @pl.when(end)
    def _():
        for k in range(N_K):
            t_copy(k).start()

    def multiply(zs, c):
        side = jnp.where((c >= OUT_AT) & (c < OUT_AT + N_OUT), 0, 1)
        acc[side, zs] += lax.dot_general(
            G[zs, :, lanes(c)], T[:, lanes(c)], NT, preferred_element_type=jnp.float32)

    per_round = N_E + N_A

    def end_z(t):
        tt = jnp.where(t < PAUSE, t, t - HOLD)
        r, i = lax.div(tt, per_round) + 1, lax.rem(tt, per_round)
        zs = jnp.where(low, r, NZ - 1 - r)
        from_own = i < N_E
        c = jnp.where(from_own, order_kept(i), A0 + i - N_E)
        xx = jnp.where(from_own, x, 1 - x)
        arrived(zs, xx, c)

        @pl.when(i < N_B)
        def _():
            piece(2, zs, xx, c).start()

        @pl.when(i >= N_E)
        def _():
            multiply(zs, c)

    def mid_outer(t):
        @pl.when(t < NC)
        def _():
            c = order_all(t)
            arrived(outward, x, c)

            @pl.when(t < N_W)
            def _():
                piece(0, outward, x, c).start()

            @pl.when(t < A0)
            def _():
                piece(2, outward, x, c).start()

        @pl.when((t >= N_W + DELAY) & (t < NC + DELAY))
        def _():
            piece(0, outward, x, order_all(t - DELAY)).start()

        @pl.when((t >= OTHER_A) & (t < OTHER_A + N_A))
        def _():
            c = A0 + t - OTHER_A
            arrived(outward, 1 - x, c)
            piece(0, outward, 1 - x, c).start()
            multiply(outward, c)

    def mid_across(t):
        s = t - NC
        mixed = 2 * (N_W + N_A)
        near = t < NC
        i_far = jnp.where(
            s < mixed - 2 * N_A, lax.div(s, 2), s - (N_W + N_A) - N_W)
        is_near_other = (s >= 0) & (
            ((s < 2 * N_W) & (lax.rem(s, 2) == 1))
            | ((s >= 2 * N_W) & (s < 2 * N_W + N_A)))
        o = jnp.where(s < 2 * N_W, lax.div(s, 2), s - N_W)
        c_other = jnp.where(o < N_A, A0 + o, order_all(o - N_A))
        u = s - (2 * N_W + N_A)
        far_w = (u >= 0) & (u < N_W)
        far_a = u >= N_W + NC - N_W
        far_other = far_w | far_a
        c_far_other = jnp.where(far_w, order_all(u), A0 + u - NC)
        c = jnp.where(
            near, order_all(t),
            jnp.where(is_near_other, c_other,
                      jnp.where(far_other, c_far_other, order_all(i_far))))
        zs = jnp.where(near | is_near_other, inward, far)
        other = is_near_other | far_other
        xx = jnp.where(other, 1 - x, x)
        arrived(zs, xx, c)
        crossing = c >= A0

        @pl.when(crossing | (jnp.logical_not(other) & (c < K0)))
        def _():
            piece(1, zs, xx, c).start()

        @pl.when(jnp.logical_not(other) & (c < M0))
        def _():
            piece(2, zs, xx, c).start()

        @pl.when(other)
        def _():
            multiply(zs, c)

    def x_step(n):
        m = n - N_E
        r = lax.div(m, N_B) + 1
        own_e = n < N_E
        z_e = jnp.where(own_e, z, jnp.where(low, r, NZ - 1 - r))
        c_e = jnp.where(
            own_e, jnp.where(n < N_A, A0 + n, order_kept(n - N_A)), order_kept(lax.rem(m, N_B)))
        m = n - NC
        v = m - N_W
        own_m = n < NC
        first = m < N_W
        pair = v < 2 * M0
        even = first | (pair & (lax.rem(v, 2) == 0))
        z_m = jnp.where(
            own_m, z, jnp.where(even, outward, jnp.where(pair, inward, far)))
        c_m = jnp.where(
            own_m, jnp.where(n < N_A, A0 + n, order_all(n - N_A)),
            jnp.where(first, order_all(m),
                      jnp.where(pair, plain(lax.div(v, 2)), plain(v - 2 * M0))))
        zs, c = jnp.where(end, z_e, z_m), jnp.where(end, c_e, c_m)
        arrived(zs, 1 - x, c)

        @pl.when((n < N_A) | (mid & (n < N_A + N_W)) | (mid & (n >= NC) & (n < NC + N_W)))
        def _():
            piece(0, zs, 1 - x, c).start()

        @pl.when(mid & (n < N_A))
        def _():
            piece(1, zs, 1 - x, c).start()

        multiply(zs, c)

    def p_copy(zs):
        return pltpu.make_async_remote_copy(
            src_ref=PS.at[zs], dst_ref=PR.at[zs], send_sem=p_send.at[zs],
            recv_sem=p_recv.at[zs], device_id=device(1), device_id_type=MESH)

    def help_end(zs):
        PA[...] = jnp.zeros_like(PA)

        def add(k, carry):
            PA[...] += lax.dot_general(
                G[zs, :, lanes(K0 + k)], TN[:, lanes(k)], NT,
                preferred_element_type=jnp.float32)
            return carry

        lax.fori_loop(0, N_K, add, 0)
        PS[zs] = PA[...].astype(jnp.bfloat16)
        p_copy(zs).start()

    def part(side, to, frm):
        buf, ssem, rsem = ((RO, ro_send, ro_recv), (RI, ri_send, ri_recv))[side]
        return pltpu.make_async_remote_copy(
            src_ref=acc.at[side, to], dst_ref=buf.at[frm], send_sem=ssem.at[to],
            recv_sem=rsem.at[frm], device_id={"hidden": to}, device_id_type=MESH)

    def send_parts(side, last):
        for to in range(NZ):
            @pl.when((h != to) & ((z_last == to) if last else (z_last != to)))
            def _(to=to):
                part(side, to, h).start()

    def summed(side):
        buf = RI if side else RO
        value = acc[side, h]
        for k in range(1, NZ):
            frm = lax.rem(h + k, NZ)
            part(side, h, frm).wait_recv()
            value = value + buf[frm]
        return value.astype(jnp.bfloat16)

    blk = acc.shape[2]

    def block_of(hh):
        return pl.ds(pl.multiple_of(hh * blk, blk), blk)

    def os_copy(xx, hh, dev, sem):
        ref = OS.at[xx, block_of(hh), :]
        return pltpu.make_async_remote_copy(
            src_ref=ref, dst_ref=ref, send_sem=sem, recv_sem=os_recv.at[xx, hh],
            device_id=dev, device_id_type=MESH)

    def is_copy(xx):
        return pltpu.make_async_remote_copy(
            src_ref=IS.at[xx], dst_ref=IS.at[xx], send_sem=is_sem.at[0],
            recv_sem=is_sem.at[1], device_id={"ctx": 1 - x}, device_id_type=MESH)

    def stages(t):
        @pl.when(t == OUT_EARLY)
        def _():
            send_parts(0, False)

        @pl.when(t == OUT_LATE)
        def _():
            send_parts(0, True)

        @pl.when(mid & (t == HELP))
        def _():
            for k in range(N_K):
                t_copy(k).wait_recv()

        @pl.when(mid & (t >= HELP) & (t < HELP + NZ))
        def _():
            k = t - HELP
            help_end(jnp.where(low, k, NZ - 1 - k))

        @pl.when(t == OUT_SUM)
        def _():
            OS[x, block_of(h), :] = summed(0)
            os_copy(x, h, {"ctx": 1 - x}, os_send.at[0]).start()
            for k in range(1, NZ):
                os_copy(x, h, {"hidden": lax.rem(h + k, NZ)}, os_send.at[k]).start()

        @pl.when(t == IN_EARLY)
        def _():
            @pl.when(end)
            def _():
                for zs in range(NZ):
                    p_copy(zs).wait_recv()
                    acc[1, zs] += PR[zs].astype(jnp.float32)

            send_parts(1, False)

        @pl.when(t == OUT_RELAY)
        def _():
            os_copy(1 - x, h, {"ctx": 1 - x}, os_send.at[0]).wait_recv()
            for k in range(1, NZ):
                os_copy(1 - x, h, {"hidden": lax.rem(h + k, NZ)}, osr_send.at[k - 1]).start()

    n_end = per_round * (NZ - 1)
    n_across = 2 * (NC + N_W + N_A)
    units_e, units_m = N_E + (NZ - 1) * N_B, NC + N_W + 3 * M0

    def body(t, carry):
        @pl.when(end & ((t < PAUSE) | ((t >= PAUSE + HOLD) & (t < n_end + HOLD))))
        def _():
            end_z(t)

        @pl.when(mid)
        def _():
            mid_outer(t)

            @pl.when(t < n_across)
            def _():
                mid_across(t)

        n = t - LAG

        @pl.when((n >= 0) & (n < jnp.where(end, units_e, units_m)))
        def _():
            x_step(n)

        stages(t)
        return carry

    lax.fori_loop(0, max(n_end + HOLD, n_across, units_e + LAG, units_m + LAG), body, 0)

    send_parts(1, True)
    IS[x] = summed(1)
    is_copy(x).start()

    for k in range(1, NZ):
        for xx in range(2):
            os_copy(xx, lax.rem(h + k, NZ), {"ctx": 1 - x}, os_send.at[0]).wait_recv()

    total = lax.dot_general(OS[x], IS[x], NT, preferred_element_type=jnp.float32)
    is_copy(1 - x).wait_recv()
    total = total + lax.dot_general(OS[1 - x], IS[1 - x], NT, preferred_element_type=jnp.float32)
    out_ref[...] = jnp.dot(
        rot_ref[...], total.astype(jnp.bfloat16), preferred_element_type=jnp.float32)

    is_copy(x).wait_send()
    for k in range(NZ):
        os_copy(x, h, {"ctx": 1 - x}, os_send.at[k]).wait_send()
        if k:
            os_copy(x, h, {"ctx": 1 - x}, osr_send.at[k - 1]).wait_send()
    for to in range(NZ):
        @pl.when(h != to)
        def _(to=to):
            part(0, to, h).wait_send()
            part(1, to, h).wait_send()

    @pl.when(end)
    def _():
        sent(0, z, x, 0, NC)
        sent(0, z, 1 - x, A0, NC)
        for k in range(N_K):
            t_copy(k).wait_send()
        sent(2, z, x, 0, K0)
        sent(2, z, x, A0, NC)
        for r in range(1, NZ):
            sent(2, jnp.where(low, r, NZ - 1 - r), x, 0, K0)

    @pl.when(mid)
    def _():
        for zs in (z, outward):
            sent(0, zs, x, 0, NC)
            sent(0, zs, 1 - x, M0, NC)
        for zs in (z, inward, far):
            sent(1, zs, x, 0, K0)
            sent(1, zs, x, A0, NC)
            sent(1, zs, 1 - x, A0, NC)
        sent(2, z, x, 0, NC)
        sent(2, outward, x, 0, A0)
        sent(2, inward, x, 0, M0)
        sent(2, far, x, 0, M0)
        for zs in range(NZ):
            p_copy(zs).wait_send()


def fast(activations, out_grads, input_basis, output_basis, rotation):
    tokens = activations.reshape(-1, activations.shape[-1])
    grad_rows = out_grads.reshape(-1, out_grads.shape[-1])
    d_in, d_out = tokens.shape[1], grad_rows.shape[1]
    width = d_in + d_out
    m = tokens.shape[0]
    w = input_basis.shape[1]
    rank = rotation.shape[1]
    blk = 2 * w
    dma = pltpu.SemaphoreType.DMA
    f32, bf16 = jnp.float32, jnp.bfloat16
    anym = pl.BlockSpec(memory_space=pl.ANY)
    vmem = pl.BlockSpec(memory_space=pltpu.VMEM)
    logged = pl.pallas_call(
        kernel,
        out_shape=jax.ShapeDtypeStruct((rotation.shape[0], blk), f32),
        in_specs=[anym, anym, anym, anym, vmem],
        out_specs=vmem,
        scratch_shapes=[
            pltpu.VMEM((NZ, blk, width), bf16),
            pltpu.VMEM((m, width), bf16),
            pltpu.VMEM((2, NZ, blk, m), f32),
            pltpu.VMEM((NZ, blk, m), f32),
            pltpu.VMEM((NZ, blk, m), f32),
            pltpu.VMEM((2, rank, m), bf16),
            pltpu.VMEM((2, blk, m), bf16),
            pltpu.VMEM((m, width // NC * N_K), bf16),
            pltpu.VMEM((blk, m), f32),
            pltpu.VMEM((NZ, blk, m), bf16),
            pltpu.VMEM((NZ, blk, m), bf16),
            dma((3,)), dma((3,)), dma((NZ, 2, NC)), dma((3, NZ, 2)),
            dma((NZ,)), dma((NZ,)), dma((NZ,)), dma((NZ,)),
            dma((2, NZ)), dma((NZ,)), dma((NZ,)), dma((2,)),
            dma((N_K,)), dma((N_K,)), dma((NZ,)), dma((NZ,)),
        ],
        compiler_params=pltpu.CompilerParams(
            collective_id=0, has_side_effects=True, vmem_limit_bytes=60 * 2**20),
    )(tokens, grad_rows, input_basis.T, output_basis.T, rotation)
    return logged.reshape(1, logged.shape[0], logged.shape[1])


def solution(mesh):
    size = mesh.shape

    def program(activations, out_grads, input_basis, output_basis, rotation):
        fits = (
            size["dp"] == NZ and size["hidden"] == NZ and size["ctx"] == 2
            and out_grads.shape[2] % (128 * N_OUT * NZ) == 0
            and activations.shape[2] * N_OUT == out_grads.shape[2] * (NC - N_OUT)
        )
        return jax.shard_map(
            fast if fits else local,
            mesh=mesh,
            in_specs=(
                P("dp", "ctx", "hidden"),
                P("dp", "ctx", "hidden"),
                P("hidden", ("dp", "ctx")),
                P("hidden", ("dp", "ctx")),
                P("ctx", None),
            ),
            out_specs=P("dp", "ctx", "hidden"),
            check_vma=False,
        )(activations, out_grads, input_basis, output_basis, rotation)

    return program
```

time: 195 us -> 180 us (0.923); the launches traced: 193 us -> 180 us
  Pallas kernels: 191 us -> 179 us
    pallas_call x1, Pallas kernels: 191 us -> 179 us  [fast(): pl.pallas_call(kernel, out_shape=jax.ShapeDtypeStruct((rotation.shape[0],...]
where the time goes in v2:
time: 180 us
  Pallas kernels  179 us (99%)
    pallas_call x1, Pallas kernels, fast(): pl.pallas_call(kernel, out_shape=jax.ShapeDtypeStruct((rotation.shape[0],...  179 us

profile of v2, /device:TPU:5, one launch (start us, length us, event | category | flops | bytes accessed | tf_op | source)
XLA Modules:
  0.0 180.2 jit_solution(11156430079439638912)
XLA Ops:
  0.0 178.6 %shard_map.55 = f32[256,128]{1,0:T(8,128)} custom-call(bf16[512,13312]{1,0:T(8,128)(2,1)} %bitcast.5, bf16[512,4096]{1,0:T(8,128)(2,1)} %bitcast.6, bf16[64,13312]{1,0:T(8,128)(2,1)} %bitcast.7, bf16[64,4096]{1,0:T(8,128)(2,1)} %bitcast.9, bf16[256,512]{1,0:T(8,128)(2,1)} %rot_ref.1), custom_call_target="tpu_custom_call" | custom-call | tf_op jit(solution)/shard_map/pallas_call | solution.py:496
  178.6 1.6 copy.7

commit v3 on v2

--- a/solution.py
+++ b/solution.py
@@ -23,7 +23,8 @@
 LAG = 1
 DELAY = 18
 PAUSE, HOLD = 35, 4
-OUT_EARLY, HELP, OUT_LATE, OTHER_A, OUT_SUM, IN_EARLY, OUT_RELAY = 34, 42, 43, 45, 47, 48, 50
+MOVE, IN_FIRST, OUT_EARLY, OTHER_A, IN_SECOND = N_A + LAG, 28, 34, 35, 42
+HELP, OUT_LATE, OUT_SUM, HELP_SUM, OUT_RELAY = 43, 43, 47, 50, 50
 
 
 def outer_sum(left, right):
@@ -58,11 +59,11 @@
 
 def kernel(
     act_hbm, grad_hbm, bi_hbm, bo_hbm, rot_ref, out_ref,
-    G, T, acc, RO, RI, OS, IS, TN, PA, PS, PR,
+    G, T, acc, RO, RI, OS, IS, TN, PA, PS, PQ, PT, PR,
     load_sem, own_sem, g_recv, g_send,
     ro_recv, ro_send, ri_recv, ri_send,
     os_recv, os_send, osr_send, is_sem,
-    t_recv, t_send, p_recv, p_send,
+    t_recv, t_send, p_recv, p_send, pt_sem,
 ):
     z, x, h = lax.axis_index("dp"), lax.axis_index("ctx"), lax.axis_index("hidden")
     chunk = G.shape[2] // NC
@@ -177,11 +178,6 @@
     acc[...] = jnp.zeros_like(acc)
     for copy in load:
         copy.wait()
-
-    @pl.when(end)
-    def _():
-        for k in range(N_K):
-            t_copy(k).start()
 
     def multiply(zs, c):
         side = jnp.where((c >= OUT_AT) & (c < OUT_AT + N_OUT), 0, 1)
@@ -302,23 +298,40 @@
 
         multiply(zs, c)
 
-    def p_copy(zs):
-        return pltpu.make_async_remote_copy(
-            src_ref=PS.at[zs], dst_ref=PR.at[zs], send_sem=p_send.at[zs],
-            recv_sem=p_recv.at[zs], device_id=device(1), device_id_type=MESH)
+    def p_copy(to, frm):
+        return pltpu.make_async_remote_copy(
+            src_ref=PS.at[to], dst_ref=PQ.at[frm], send_sem=p_send.at[to],
+            recv_sem=p_recv.at[frm], device_id={"hidden": to}, device_id_type=MESH)
+
+    def pt_copy(way):
+        return pltpu.make_async_remote_copy(
+            src_ref=PT, dst_ref=PR, send_sem=pt_sem.at[0], recv_sem=pt_sem.at[1],
+            device_id=device(way), device_id_type=MESH)
 
     def help_end(zs):
-        PA[...] = jnp.zeros_like(PA)
+        PA[zs] = jnp.zeros_like(PA[zs])
 
         def add(k, carry):
-            PA[...] += lax.dot_general(
+            PA[zs] += lax.dot_general(
                 G[zs, :, lanes(K0 + k)], TN[:, lanes(k)], NT,
                 preferred_element_type=jnp.float32)
             return carry
 
         lax.fori_loop(0, N_K, add, 0)
-        PS[zs] = PA[...].astype(jnp.bfloat16)
-        p_copy(zs).start()
+
+        @pl.when(zs != h)
+        def _():
+            PS[zs] = PA[zs].astype(jnp.bfloat16)
+            p_copy(zs, h).start()
+
+    def help_sum():
+        value = PA[h]
+        for k in range(1, NZ):
+            frm = lax.rem(h + k, NZ)
+            p_copy(h, frm).wait_recv()
+            value = value + PQ[frm].astype(jnp.float32)
+        PT[...] = value.astype(jnp.bfloat16)
+        pt_copy(1).start()
 
     def part(side, to, frm):
         buf, ssem, rsem = ((RO, ro_send, ro_recv), (RI, ri_send, ri_recv))[side]
@@ -326,11 +339,23 @@
             src_ref=acc.at[side, to], dst_ref=buf.at[frm], send_sem=ssem.at[to],
             recv_sem=rsem.at[frm], device_id={"hidden": to}, device_id_type=MESH)
 
-    def send_parts(side, last):
+    def send_parts(side, which):
         for to in range(NZ):
-            @pl.when((h != to) & ((z_last == to) if last else (z_last != to)))
+            @pl.when((h != to) & which(to))
             def _(to=to):
                 part(side, to, h).start()
+
+    def is_last(to):
+        return z_last == to
+
+    def not_last(to):
+        return z_last != to
+
+    def is_first(to):
+        return (z == to) | (end & (inward == to))
+
+    def is_second(to):
+        return (z_last != to) & (z != to) & (mid | (inward != to))
 
     def summed(side):
         buf = RI if side else RO
@@ -358,13 +383,18 @@
             recv_sem=is_sem.at[1], device_id={"ctx": 1 - x}, device_id_type=MESH)
 
     def stages(t):
+        @pl.when(end & (t == MOVE))
+        def _():
+            for k in range(N_K):
+                t_copy(k).start()
+
         @pl.when(t == OUT_EARLY)
         def _():
-            send_parts(0, False)
+            send_parts(0, not_last)
 
         @pl.when(t == OUT_LATE)
         def _():
-            send_parts(0, True)
+            send_parts(0, is_last)
 
         @pl.when(mid & (t == HELP))
         def _():
@@ -383,15 +413,17 @@
             for k in range(1, NZ):
                 os_copy(x, h, {"hidden": lax.rem(h + k, NZ)}, os_send.at[k]).start()
 
-        @pl.when(t == IN_EARLY)
-        def _():
-            @pl.when(end)
-            def _():
-                for zs in range(NZ):
-                    p_copy(zs).wait_recv()
-                    acc[1, zs] += PR[zs].astype(jnp.float32)
-
-            send_parts(1, False)
+        @pl.when(t == IN_FIRST)
+        def _():
+            send_parts(1, is_first)
+
+        @pl.when(t == IN_SECOND)
+        def _():
+            send_parts(1, is_second)
+
+        @pl.when(mid & (t == HELP_SUM))
+        def _():
+            help_sum()
 
         @pl.when(t == OUT_RELAY)
         def _():
@@ -427,7 +459,13 @@
 
     lax.fori_loop(0, max(n_end + HOLD, n_across, units_e + LAG, units_m + LAG), body, 0)
 
-    send_parts(1, True)
+    send_parts(1, is_last)
+
+    @pl.when(end)
+    def _():
+        pt_copy(0).wait_recv()
+        acc[1, h] += PR[...].astype(jnp.float32)
+
     IS[x] = summed(1)
     is_copy(x).start()
 
@@ -476,8 +514,11 @@
         sent(2, outward, x, 0, A0)
         sent(2, inward, x, 0, M0)
         sent(2, far, x, 0, M0)
-        for zs in range(NZ):
-            p_copy(zs).wait_send()
+        for to in range(NZ):
+            @pl.when(h != to)
+            def _(to=to):
+                p_copy(to, h).wait_send()
+        pt_copy(1).wait_send()
 
 
 def fast(activations, out_grads, input_basis, output_basis, rotation):
@@ -507,13 +548,15 @@
             pltpu.VMEM((2, rank, m), bf16),
             pltpu.VMEM((2, blk, m), bf16),
             pltpu.VMEM((m, width // NC * N_K), bf16),
-            pltpu.VMEM((blk, m), f32),
+            pltpu.VMEM((NZ, blk, m), f32),
             pltpu.VMEM((NZ, blk, m), bf16),
             pltpu.VMEM((NZ, blk, m), bf16),
+            pltpu.VMEM((blk, m), bf16),
+            pltpu.VMEM((blk, m), bf16),
             dma((3,)), dma((3,)), dma((NZ, 2, NC)), dma((3, NZ, 2)),
             dma((NZ,)), dma((NZ,)), dma((NZ,)), dma((NZ,)),
             dma((2, NZ)), dma((NZ,)), dma((NZ,)), dma((2,)),
-            dma((N_K,)), dma((N_K,)), dma((NZ,)), dma((NZ,)),
+            dma((N_K,)), dma((N_K,)), dma((NZ,)), dma((NZ,)), dma((2,)),
         ],
         compiler_params=pltpu.CompilerParams(
             collective_id=0, has_side_effects=True, vmem_limit_bytes=60 * 2**20),

time: 180 us -> 170 us (0.944)
  Pallas kernels: 179 us -> 167 us
    pallas_call x1, Pallas kernels: 179 us -> 167 us  [fast(): pl.pallas_call(kernel, out_shape=jax.ShapeDtypeStruct((rotation.shape[0],...]
where the time goes in v3:
time: 170 us; the launch traced here: 169 us
  Pallas kernels  167 us (98%)
    pallas_call x1, Pallas kernels, fast(): pl.pallas_call(kernel, out_shape=jax.ShapeDtypeStruct((rotation.shape[0],...  167 us

profile of v3, /device:TPU:5, one launch (start us, length us, event | category | flops | bytes accessed | tf_op | source)
XLA Modules:
  0.0 168.8 jit_solution(13953122328960220800)
XLA Ops:
  0.0 167.2 %shard_map.55 = f32[256,128]{1,0:T(8,128)} custom-call(bf16[512,13312]{1,0:T(8,128)(2,1)} %bitcast.5, bf16[512,4096]{1,0:T(8,128)(2,1)} %bitcast.6, bf16[64,13312]{1,0:T(8,128)(2,1)} %bitcast.7, bf16[64,4096]{1,0:T(8,128)(2,1)} %bitcast.9, bf16[256,512]{1,0:T(8,128)(2,1)} %rot_ref.1), custom_call_target="tpu_custom_call" | custom-call | tf_op jit(solution)/shard_map/pallas_call | solution.py:537
  167.2 1.6 copy.7
